TPU v7x, 32 devices: a whole 2x2x4 slice. The times are simulated.
32 devices in a mesh: tm: 4 (over y, core), chan: 8 (over z, x).
Axes of the slice: x: 2, y: 2, z: 4, core: 2. Of those that a mesh axis runs over, the one named last changes fastest.
Arguments:
- traces: bfloat16 [8, 1024, 1024], P('tm', 'chan'), may hold values from -6 to 6
- lengths: int32 [8], replicated, may hold values from 512 to 1024
- source_blocks: int32 [3], replicated, may hold values from 0 to 31
Outputs:
- stacks: float32 [32, 3, 201, 1024], P('tm', None, None, 'chan')
Inputs may be any that keep to these rules, and one draw needn't show every extreme that they name: Step s takes the source channels 32 * source_blocks[s] to 32 * source_blocks[s] + 31. `lengths`: samples at and after a segment's length are not used.
All inputs are finite; a program needn't handle non-finite values.
Results may differ from a plain program's by a relative error of at most 0.0085.
Values may be sent and summed in bfloat16 or wider, within the bound.
No kernel may reach another device: no remote copies, remote signals or barrier semaphores. Data moves between devices by JAX's collectives and lax.ppermute only.
A program may use at most 256 MiB of HBM per device.

v0:
```python
import jax
import jax.numpy as jnp
from jax import lax
from jax.sharding import PartitionSpec as P

MAXLAG = 100
SRC = 32
epsilon = 1e-06


def whiten(traces, lengths):
    sample_len = traces.shape[2]
    positions = lax.broadcasted_iota(jnp.int32, (1, 1, sample_len), 2)
    valid_mask = (positions < lengths[:, None, None]).astype(jnp.float32)
    masked = traces.astype(jnp.float32) * valid_mask
    seg_count = lengths.astype(jnp.float32)[:, None, None]
    mean_power = jnp.sum(masked * masked, axis=2, keepdims=True) / seg_count
    return (masked / jnp.sqrt(mean_power + epsilon)).astype(jnp.bfloat16)


def correlate(sources, receivers, lengths):
    sample_len = sources.shape[2]
    padded = jnp.pad(sources, ((0, 0), (0, 0), (MAXLAG, MAXLAG)))
    root_count = jnp.sqrt(lengths.astype(jnp.float32))
    lag_total = 2 * MAXLAG + 1
    lag_blocks = []
    for start_lag in range(0, lag_total, 67):
        lag_width = min(67, lag_total - start_lag)
        offsets = start_lag + jnp.arange(lag_width, dtype=jnp.int32)

        def take_lag(lag_value):
            return lax.dynamic_slice_in_dim(padded, 2 * MAXLAG - lag_value, sample_len, 2)

        shifted = jax.vmap(take_lag, out_axes=2)(offsets)
        product = jnp.einsum(
            "gnau,gcu->gnac", shifted, receivers, preferred_element_type=jnp.float32
        )
        lag_blocks.append(jnp.sum(product / root_count[:, None, None, None], axis=0))
    return jnp.concatenate(lag_blocks, axis=1)


def shards(traces, lengths, source_blocks):
    seg_dev = traces.shape[0]
    own_lengths = lax.dynamic_slice_in_dim(lengths, lax.axis_index("tm") * seg_dev, seg_dev, 0)
    whitened = whiten(traces, own_lengths)
    per_owner = whitened.shape[1] // SRC
    step_count = source_blocks.shape[0]
    sources = []
    my_index = lax.axis_index("chan")
    contributions = []
    for step_index in range(step_count):
        owner_index = source_blocks[step_index] // per_owner
        local_start = source_blocks[step_index] % per_owner * SRC
        block_here = lax.dynamic_slice_in_dim(whitened, local_start, SRC, 1).astype(jnp.float32)
        contributions.append(
            jnp.where(owner_index == my_index, block_here, jnp.zeros_like(block_here))
        )
    summed = lax.psum(jnp.stack(contributions), "chan")
    sources = [summed[step_index].astype(jnp.bfloat16) for step_index in range(step_count)]
    results = []
    for step_index in range(step_count):
        chosen = sources[step_index]
        results.append(
            lax.psum_scatter(
                correlate(chosen, whitened, own_lengths).astype(jnp.bfloat16),
                "tm",
                scatter_dimension=0,
                tiled=True,
            ).astype(jnp.float32)
        )
    return jnp.stack(results, axis=1)


def solution(mesh):
    return jax.shard_map(
        shards,
        mesh=mesh,
        in_specs=(P("tm", "chan", None), P(), P()),
        out_specs=P("tm", None, None, "chan"),
        check_vma=False,
    )
```

profile of v0, /device:TPU:0, one launch (start us, length us, event | category | flops | bytes accessed | tf_op | source)
XLA Modules:
  0.0 1519.1 jit_solution(4298698127265527890)
XLA Ops:
  19.2 47.3 %all-reduce.14 = bf16[3,2,32,1024]{3,2,1,0:T(8,128)(2,1)S(1)} all-reduce(f32[3,2,32,1024]{3,2,1,0:T(8,128)S(1)} %pad_maximum_fusion.3), channel_id=1, replica_groups=mesh['tm'=4,'chan'=8] {'chan'}, use_global_device_ids=true, to_apply=%region_1.2 | all-reduce | flops 196608 | bytes 1179648 | tf_op jit(solution)/shard_map/psum | solution.py:58
  66.7 4.5 broadcast.153.clone
  71.2 128.9 %while.9 = (s32[]{:T(128)}, bf16[2,32,1224]{2,1,0:T(8,128)(2,1)S(1)}, s32[67,3]{0,1:T(4,128)S(1)}, bf16[67,2,32,1024]{3,2,1,0:T(8,128)(2,1)}, s32[]{:T(128)}) while((s32[]{:T(128)}, bf16[2,32,1224]{2,1,0:T(8,128)(2,1)S(1)}, s32[67,3]{0,1:T(4,128)S(1)}, bf16[67,2,32,1024]{3,2,1,0:T(8,128)(2,1)}, s32[]{:T(128)}) %tuple.120), condition=%wide.while_cond, body=%wide.while_body.sunk | while | flops 2 | bytes 262765 | solution.py:32
  200.1 5.9 fusion.16
  206.1 4.5 broadcast.153.clone.1
  210.5 133.6 %while.10 = (s32[]{:T(128)}, bf16[2,32,1224]{2,1,0:T(8,128)(2,1)S(1)}, s32[67,3]{0,1:T(4,128)S(1)}, bf16[67,2,32,1024]{3,2,1,0:T(8,128)(2,1)}, s32[]{:T(128)}) while((s32[]{:T(128)}, bf16[2,32,1224]{2,1,0:T(8,128)(2,1)S(1)}, s32[67,3]{0,1:T(4,128)S(1)}, bf16[67,2,32,1024]{3,2,1,0:T(8,128)(2,1)}, s32[]{:T(128)}) %tuple.150), condition=%wide.while_cond.1, body=%wide.while_body.1.sunk | while | flops 2 | bytes 262765 | solution.py:32
  344.1 7.3 fusion.14
  355.9 134.0 %while.11 = (s32[]{:T(128)}, bf16[2,32,1224]{2,1,0:T(8,128)(2,1)S(1)}, s32[67,3]{0,1:T(4,128)S(1)}, bf16[67,2,32,1024]{3,2,1,0:T(8,128)(2,1)}, s32[]{:T(128)}) while((s32[]{:T(128)}, bf16[2,32,1224]{2,1,0:T(8,128)(2,1)S(1)}, s32[67,3]{0,1:T(4,128)S(1)}, bf16[67,2,32,1024]{3,2,1,0:T(8,128)(2,1)}, s32[]{:T(128)}) %tuple.151), condition=%wide.while_cond.2, body=%wide.while_body.2.sunk | while | flops 2 | bytes 262765 | solution.py:32
  489.9 7.4 fusion.12
  497.4 4.5 broadcast.153.clone.3
  501.9 128.0 %while.12 = (s32[]{:T(128)}, bf16[2,32,1224]{2,1,0:T(8,128)(2,1)S(1)}, s32[67,3]{0,1:T(4,128)S(1)}, bf16[67,2,32,1024]{3,2,1,0:T(8,128)(2,1)}, s32[]{:T(128)}) while((s32[]{:T(128)}, bf16[2,32,1224]{2,1,0:T(8,128)(2,1)S(1)}, s32[67,3]{0,1:T(4,128)S(1)}, bf16[67,2,32,1024]{3,2,1,0:T(8,128)(2,1)}, s32[]{:T(128)}) %tuple.156), condition=%wide.while_cond.3, body=%wide.while_body.3.sunk | while | flops 2 | bytes 262765 | solution.py:32
  629.8 7.3 fusion.10
  641.7 141.5 %while.13 = (s32[]{:T(128)}, bf16[2,32,1224]{2,1,0:T(8,128)(2,1)S(1)}, s32[67,3]{0,1:T(4,128)S(1)}, bf16[67,2,32,1024]{3,2,1,0:T(8,128)(2,1)}, s32[]{:T(128)}) while((s32[]{:T(128)}, bf16[2,32,1224]{2,1,0:T(8,128)(2,1)S(1)}, s32[67,3]{0,1:T(4,128)S(1)}, bf16[67,2,32,1024]{3,2,1,0:T(8,128)(2,1)}, s32[]{:T(128)}) %tuple.158), condition=%wide.while_cond.4, body=%wide.while_body.4.sunk | while | flops 2 | bytes 262765 | solution.py:32
  783.1 7.3 fusion.8
  794.9 134.6 %while.14 = (s32[]{:T(128)}, bf16[2,32,1224]{2,1,0:T(8,128)(2,1)S(1)}, s32[67,3]{0,1:T(4,128)S(1)}, bf16[67,2,32,1024]{3,2,1,0:T(8,128)(2,1)}, s32[]{:T(128)}) while((s32[]{:T(128)}, bf16[2,32,1224]{2,1,0:T(8,128)(2,1)S(1)}, s32[67,3]{0,1:T(4,128)S(1)}, bf16[67,2,32,1024]{3,2,1,0:T(8,128)(2,1)}, s32[]{:T(128)}) %tuple.160), condition=%wide.while_cond.5, body=%wide.while_body.5.sunk | while | flops 2 | bytes 262765 | solution.py:32
  929.6 7.3 fusion.6
  941.5 132.3 %while.15 = (s32[]{:T(128)}, bf16[2,32,1224]{2,1,0:T(8,128)(2,1)S(1)}, s32[67,3]{0,1:T(4,128)S(1)}, bf16[67,2,32,1024]{3,2,1,0:T(8,128)(2,1)}, s32[]{:T(128)}) while((s32[]{:T(128)}, bf16[2,32,1224]{2,1,0:T(8,128)(2,1)S(1)}, s32[67,3]{0,1:T(4,128)S(1)}, bf16[67,2,32,1024]{3,2,1,0:T(8,128)(2,1)}, s32[]{:T(128)}) %tuple.157), condition=%wide.while_cond.6, body=%wide.while_body.6.sunk | while | flops 2 | bytes 262765 | solution.py:32
  1073.7 7.3 fusion.4
  1085.5 141.9 %while.16 = (s32[]{:T(128)}, bf16[2,32,1224]{2,1,0:T(8,128)(2,1)S(1)}, s32[67,3]{0,1:T(4,128)S(1)}, bf16[67,2,32,1024]{3,2,1,0:T(8,128)(2,1)}, s32[]{:T(128)}) while((s32[]{:T(128)}, bf16[2,32,1224]{2,1,0:T(8,128)(2,1)S(1)}, s32[67,3]{0,1:T(4,128)S(1)}, bf16[67,2,32,1024]{3,2,1,0:T(8,128)(2,1)}, s32[]{:T(128)}) %tuple.159), condition=%wide.while_cond.7, body=%wide.while_body.7.sunk | while | flops 2 | bytes 262765 | solution.py:32
  1227.4 7.3 fusion.2
  1239.2 134.3 %while.17 = (s32[]{:T(128)}, bf16[2,32,1224]{2,1,0:T(8,128)(2,1)S(1)}, s32[67,3]{0,1:T(4,128)S(1)}, bf16[67,2,32,1024]{3,2,1,0:T(8,128)(2,1)}, s32[]{:T(128)}) while((s32[]{:T(128)}, bf16[2,32,1224]{2,1,0:T(8,128)(2,1)S(1)}, s32[67,3]{0,1:T(4,128)S(1)}, bf16[67,2,32,1024]{3,2,1,0:T(8,128)(2,1)}, s32[]{:T(128)}) %tuple.161), condition=%wide.while_cond.8, body=%wide.while_body.8.sunk | while | flops 2 | bytes 262765 | solution.py:32
  1373.5 7.5 fusion
  1381.0 21.9 %fusion.26 = (bf16[32,67,128]{2,1,0:T(8,128)(2,1)S(1)}, bf16[32,67,128]{2,1,0:T(8,128)(2,1)S(1)}, bf16[32,67,128]{2,1,0:T(8,128)(2,1)S(1)}, bf16[32,67,128]{2,1,...) fusion(f32[2,32,67,128]{3,1,2,0:T(8,128)S(1)} %fusion.16, ...), kind=kLoop, calls=%fused_computation.53 | loop fusion | flops 7409664 | bytes 24698888 | tf_op jit(solution)/shard_map/reduce_sum | solution.py:38
  1410.6 96.7 %all-reduce.13.cloned.1.call-done = (bf16[32,201,128]{2,0,1:T(8,128)(2,1)}, bf16[32,201,128]{2,0,1:T(8,128)(2,1)}, bf16[32,201,128]{2,0,1:T(8,128)(2,1)}) async-done(((bf16[32,201,128]{2,0,1:T(8,128)(2,1)}, bf16[32,201,128]{2,0,1:T(8,128)(2,1)}, bf16[32,201,128]{2,0,1:T(8,128)(2,1)}), (bf16[32,201,128]{2,0,1:T(8,128)(2,1)}, bf16[32,201,128]{2,0,1:T(8,128)(2,1)}, ...) | async-done | bytes 4939792
  (1852 shorter events, 1251.2 us)
Async XLA Ops:
  6.5 1500.7 %all-reduce.13.cloned.1.call-start = ((), (), s32[]{:S(2)}) async-start(), calls=%async_computation | async-start | bytes 9879552
  1373.5 7.5 copy-start
  1373.5 7.5 copy-start.1
  1405.0 4.2 copy-start.2
Sparse Core Ops, SparseCore 0:
  1409.3 97.8 all-reduce.12
where the time goes:
time: 1530 us; the launch traced here: 1520 us
  local copies, waits for them, and re-layouts  1260 us (82%)
  waiting for transfers between devices  96.7 us (6%)
  matrix products  64.6 us (4%)
  blocking collectives  47.3 us (3%)
  other arithmetic  28.4 us (2%)
  between operations  22.2 us (1%)
    gather x1809, local copies, waits for them, and re-layouts  1210 us
    unnamed x2, waiting for transfers between devices  96.7 us
    dot_general x9, matrix products, correlate(): jnp.einsum('gnau,gcu->gnac', shifted, receivers, preferred_element_type=j...  64.6 us
    psum x1, blocking collectives, shards(): summed = lax.psum(jnp.stack(contributions), 'chan')  47.3 us
    unnamed x16, local copies, waits for them, and re-layouts  41.1 us
  transfers between devices with their start and end apart: 1, of which 1 were waited for; matrix products, arithmetic and copies ran while one was open for 0% of the time, Pallas kernels for 0%

commit v1 on v0

--- a/solution.py
+++ b/solution.py
@@ -55,7 +55,8 @@
         contributions.append(
             jnp.where(owner_index == my_index, block_here, jnp.zeros_like(block_here))
         )
-    summed = lax.psum(jnp.stack(contributions), "chan")
+    xin = jnp.stack(contributions)
+    summed = jnp.sum(lax.all_gather(xin, "chan"), 0)
     sources = [summed[step_index].astype(jnp.bfloat16) for step_index in range(step_count)]
     results = []
     for step_index in range(step_count):

time: 1530 us -> 1600 us (1.046)
  waiting for transfers between devices: 96.7 us -> 196 us
  blocking collectives: 47.3 us -> 0 us
    all_gather x0 -> x1, waiting for transfers between devices: none -> 101 us  [shards(): summed = jnp.sum(lax.all_gather(xin, 'chan'), 0)]
    psum x1 -> x0, blocking collectives: 47.3 us -> none  [shards(): summed = lax.psum(jnp.stack(contributions), 'chan')]
    unnamed x2 -> x3, waiting for transfers between devices: 96.7 us -> 94.7 us
  transfers between devices with their start and end apart: 1 -> 2, of which waited for: 1 -> 2; matrix products, arithmetic and copies ran while one was open for 0% -> 0% of each run, Pallas kernels for 0% -> 0%
where the time goes in v1:
time: 1600 us; the launch traced here: 1580 us
  local copies, waits for them, and re-layouts  1260 us (79%)
  waiting for transfers between devices  196 us (12%)
  matrix products  64.7 us (4%)
  other arithmetic  32.8 us (2%)
  between operations  22.3 us (1%)
    gather x1809, local copies, waits for them, and re-layouts  1210 us
    all_gather x1, waiting for transfers between devices, shards(): summed = jnp.sum(lax.all_gather(xin, 'chan'), 0)  101 us
    unnamed x3, waiting for transfers between devices  94.7 us
    dot_general x9, matrix products, correlate(): jnp.einsum('gnau,gcu->gnac', shifted, receivers, preferred_element_type=j...  64.7 us
    unnamed x16, local copies, waits for them, and re-layouts  41.1 us
  transfers between devices with their start and end apart: 2, of which 2 were waited for; matrix products, arithmetic and copies ran while one was open for 0% of the time, Pallas kernels for 0%

profile of v1, /device:TPU:0, one launch (start us, length us, event | category | flops | bytes accessed | tf_op | source)
XLA Modules:
  0.0 1580.3 jit_solution(1712596574960141180)
XLA Ops:
  20.2 101.4 %all-gather.3.cloned.1.call-done = f32[24,2,32,1024]{3,2,1,0:T(8,128)} async-done(((f32[3,2,32,1024]{3,2,1,0:T(8,128)}), f32[24,2,32,1024]{3,2,1,0:T(8,128)}) %all-gather.3.cloned.1.call-update) | async-done | bytes 6291472 | tf_op jit(solution)/shard_map/all_gather | solution.py:59
  125.3 4.5 broadcast.153.clone
  129.8 133.6 %while.9 = (s32[]{:T(128)}, bf16[2,32,1224]{2,1,0:T(8,128)(2,1)S(1)}, s32[67,3]{0,1:T(4,128)S(1)}, bf16[67,2,32,1024]{3,2,1,0:T(8,128)(2,1)}, s32[]{:T(128)}) while((s32[]{:T(128)}, bf16[2,32,1224]{2,1,0:T(8,128)(2,1)S(1)}, s32[67,3]{0,1:T(4,128)S(1)}, bf16[67,2,32,1024]{3,2,1,0:T(8,128)(2,1)}, s32[]{:T(128)}) %tuple.120), condition=%wide.while_cond, body=%wide.while_body.sunk | while | flops 2 | bytes 262765 | solution.py:32
  263.4 5.9 fusion.16
  269.3 4.5 broadcast.153.clone.1
  273.8 133.6 %while.10 = (s32[]{:T(128)}, bf16[2,32,1224]{2,1,0:T(8,128)(2,1)S(1)}, s32[67,3]{0,1:T(4,128)S(1)}, bf16[67,2,32,1024]{3,2,1,0:T(8,128)(2,1)}, s32[]{:T(128)}) while((s32[]{:T(128)}, bf16[2,32,1224]{2,1,0:T(8,128)(2,1)S(1)}, s32[67,3]{0,1:T(4,128)S(1)}, bf16[67,2,32,1024]{3,2,1,0:T(8,128)(2,1)}, s32[]{:T(128)}) %tuple.154), condition=%wide.while_cond.1, body=%wide.while_body.1.sunk | while | flops 2 | bytes 262765 | solution.py:32
  407.4 7.3 fusion.14
  419.2 134.0 %while.11 = (s32[]{:T(128)}, bf16[2,32,1224]{2,1,0:T(8,128)(2,1)S(1)}, s32[67,3]{0,1:T(4,128)S(1)}, bf16[67,2,32,1024]{3,2,1,0:T(8,128)(2,1)}, s32[]{:T(128)}) while((s32[]{:T(128)}, bf16[2,32,1224]{2,1,0:T(8,128)(2,1)S(1)}, s32[67,3]{0,1:T(4,128)S(1)}, bf16[67,2,32,1024]{3,2,1,0:T(8,128)(2,1)}, s32[]{:T(128)}) %tuple.155), condition=%wide.while_cond.2, body=%wide.while_body.2.sunk | while | flops 2 | bytes 262765 | solution.py:32
  553.1 7.4 fusion.12
  560.6 4.5 broadcast.153.clone.3
  565.1 128.0 %while.12 = (s32[]{:T(128)}, bf16[2,32,1224]{2,1,0:T(8,128)(2,1)S(1)}, s32[67,3]{0,1:T(4,128)S(1)}, bf16[67,2,32,1024]{3,2,1,0:T(8,128)(2,1)}, s32[]{:T(128)}) while((s32[]{:T(128)}, bf16[2,32,1224]{2,1,0:T(8,128)(2,1)S(1)}, s32[67,3]{0,1:T(4,128)S(1)}, bf16[67,2,32,1024]{3,2,1,0:T(8,128)(2,1)}, s32[]{:T(128)}) %tuple.162), condition=%wide.while_cond.3, body=%wide.while_body.3.sunk | while | flops 2 | bytes 262765 | solution.py:32
  693.1 7.3 fusion.10
  704.9 141.5 %while.13 = (s32[]{:T(128)}, bf16[2,32,1224]{2,1,0:T(8,128)(2,1)S(1)}, s32[67,3]{0,1:T(4,128)S(1)}, bf16[67,2,32,1024]{3,2,1,0:T(8,128)(2,1)}, s32[]{:T(128)}) while((s32[]{:T(128)}, bf16[2,32,1224]{2,1,0:T(8,128)(2,1)S(1)}, s32[67,3]{0,1:T(4,128)S(1)}, bf16[67,2,32,1024]{3,2,1,0:T(8,128)(2,1)}, s32[]{:T(128)}) %tuple.160), condition=%wide.while_cond.4, body=%wide.while_body.4.sunk | while | flops 2 | bytes 262765 | solution.py:32
  846.4 7.3 fusion.8
  858.2 134.6 %while.14 = (s32[]{:T(128)}, bf16[2,32,1224]{2,1,0:T(8,128)(2,1)S(1)}, s32[67,3]{0,1:T(4,128)S(1)}, bf16[67,2,32,1024]{3,2,1,0:T(8,128)(2,1)}, s32[]{:T(128)}) while((s32[]{:T(128)}, bf16[2,32,1224]{2,1,0:T(8,128)(2,1)S(1)}, s32[67,3]{0,1:T(4,128)S(1)}, bf16[67,2,32,1024]{3,2,1,0:T(8,128)(2,1)}, s32[]{:T(128)}) %tuple.158), condition=%wide.while_cond.5, body=%wide.while_body.5.sunk | while | flops 2 | bytes 262765 | solution.py:32
  992.8 7.3 fusion.6
  1004.7 132.3 %while.15 = (s32[]{:T(128)}, bf16[2,32,1224]{2,1,0:T(8,128)(2,1)S(1)}, s32[67,3]{0,1:T(4,128)S(1)}, bf16[67,2,32,1024]{3,2,1,0:T(8,128)(2,1)}, s32[]{:T(128)}) while((s32[]{:T(128)}, bf16[2,32,1224]{2,1,0:T(8,128)(2,1)S(1)}, s32[67,3]{0,1:T(4,128)S(1)}, bf16[67,2,32,1024]{3,2,1,0:T(8,128)(2,1)}, s32[]{:T(128)}) %tuple.163), condition=%wide.while_cond.6, body=%wide.while_body.6.sunk | while | flops 2 | bytes 262765 | solution.py:32
  1137.0 7.3 fusion.4
  1148.8 141.9 %while.16 = (s32[]{:T(128)}, bf16[2,32,1224]{2,1,0:T(8,128)(2,1)S(1)}, s32[67,3]{0,1:T(4,128)S(1)}, bf16[67,2,32,1024]{3,2,1,0:T(8,128)(2,1)}, s32[]{:T(128)}) while((s32[]{:T(128)}, bf16[2,32,1224]{2,1,0:T(8,128)(2,1)S(1)}, s32[67,3]{0,1:T(4,128)S(1)}, bf16[67,2,32,1024]{3,2,1,0:T(8,128)(2,1)}, s32[]{:T(128)}) %tuple.161), condition=%wide.while_cond.7, body=%wide.while_body.7.sunk | while | flops 2 | bytes 262765 | solution.py:32
  1290.6 7.3 fusion.2
  1302.5 134.3 %while.17 = (s32[]{:T(128)}, bf16[2,32,1224]{2,1,0:T(8,128)(2,1)S(1)}, s32[67,3]{0,1:T(4,128)S(1)}, bf16[67,2,32,1024]{3,2,1,0:T(8,128)(2,1)}, s32[]{:T(128)}) while((s32[]{:T(128)}, bf16[2,32,1224]{2,1,0:T(8,128)(2,1)S(1)}, s32[67,3]{0,1:T(4,128)S(1)}, bf16[67,2,32,1024]{3,2,1,0:T(8,128)(2,1)}, s32[]{:T(128)}) %tuple.159), condition=%wide.while_cond.8, body=%wide.while_body.8.sunk | while | flops 2 | bytes 262765 | solution.py:32
  1436.7 7.5 fusion
  1444.2 21.9 %fusion.26 = (bf16[32,67,128]{2,1,0:T(8,128)(2,1)S(1)}, bf16[32,67,128]{2,1,0:T(8,128)(2,1)S(1)}, bf16[32,67,128]{2,1,0:T(8,128)(2,1)S(1)}, bf16[32,67,128]{2,1,...) fusion(f32[2,32,67,128]{3,1,2,0:T(8,128)S(1)} %fusion.16, ...), kind=kLoop, calls=%fused_computation.53 | loop fusion | flops 7409664 | bytes 24698888 | tf_op jit(solution)/shard_map/reduce_sum | solution.py:38
  1473.8 94.7 %all-reduce.12.cloned.1.call-done = (bf16[32,201,128]{2,0,1:T(8,128)(2,1)}, bf16[32,201,128]{2,0,1:T(8,128)(2,1)}, bf16[32,201,128]{2,0,1:T(8,128)(2,1)}) async-done(((bf16[32,201,128]{2,0,1:T(8,128)(2,1)}, bf16[32,201,128]{2,0,1:T(8,128)(2,1)}, bf16[32,201,128]{2,0,1:T(8,128)(2,1)}), (bf16[32,201,128]{2,0,1:T(8,128)(2,1)}, bf16[32,201,128]{2,0,1:T(8,128)(2,1)}, ...) | async-done | bytes 4939792
  (1855 shorter events, 1260.3 us)
Async XLA Ops:
  6.5 115.1 %all-gather.3.cloned.1.call-start = ((), (), s32[]{:S(2)}) async-start(), calls=%async_computation | async-start | bytes 7077888 | tf_op jit(solution)/shard_map/all_gather | solution.py:59
  20.1 1548.4 %all-reduce.12.cloned.1.call-start = ((), (), s32[]{:S(2)}) async-start(), calls=%async_computation.1 | async-start | bytes 9879552
  1436.7 7.5 copy-start
  1436.7 7.5 copy-start.1
  1468.2 4.2 copy-start.2
Sparse Core Ops, SparseCore 0:
  20.2 101.3 all-gather.2
  1472.6 95.8 all-reduce.11
